TPU v7x, 256 devices: a whole 4x4x8 slice. The times are simulated.
256 devices in a mesh: rows: 64 (over y, z, core), feat: 4 (over x).
Axes of the slice: x: 4, y: 4, z: 8, core: 2. Of those that a mesh axis runs over, the one named last changes fastest.
Arguments:
- feats: bfloat16 [256, 131072], P('feat', 'rows'), may hold values from -6 to 6
- weight: bfloat16 [256, 256], P('feat'), may hold values from -0.375 to 0.375
- bias: float32 [256], P('feat'), may hold values from -3 to 3
- tile_cols: int32 [8192], P('rows'), may hold values from 0 to 1023, as said below
- tile_values: bfloat16 [8192, 128, 128], P('rows'), may hold values from -0.1875 to 0.1875
- cotangent: bfloat16 [256, 131072], P('feat', 'rows'), may hold values from -6 to 6
Outputs:
- hidden_out: bfloat16 [256, 131072], P('feat', 'rows')
- grad_input: float32 [256, 131072], P('feat', 'rows')
- grad_weight: float32 [256, 256], P('feat')
- grad_bias: float32 [256], P('feat')
Inputs may be any that keep to these rules, and one draw needn't show every extreme that they name: `tile_cols`: column blocks of tiles. In each row block the first 4 tiles have column blocks on the same index of rows as the row block (index = column block // 16). Of the other tiles of one index of rows, at most 2 have column blocks on any one index, and in every draw one index receives exactly 2 such tiles from every index.
All inputs are finite; a program needn't handle non-finite values.
Results may differ from a plain program's by a relative error of at most 0.0058.
Values may be sent and summed in bfloat16 or wider, within the bound.
No kernel may reach another device: no remote copies, remote signals or barrier semaphores. Data moves between devices by JAX's collectives and lax.ppermute only.
A program may use at most 128 MiB of HBM per device.

v0:
```python
import math
import jax
import jax.numpy as jnp
from jax import lax
from jax.sharding import PartitionSpec as P

TL = 4


def local(feats, weight, bias, tile_cols, tile_values, cotangent):
    hid_dev = weight.shape[1] // lax.axis_size("feat")
    nodes_dev = feats.shape[1]
    block = tile_values.shape[1]
    row_blocks = nodes_dev // block
    peers = lax.axis_size("rows")
    tiles_dev = tile_cols.shape[0]
    per_block = tiles_dev // row_blocks
    remote_count = row_blocks * (per_block - TL)
    capacity = 2 * remote_count // peers
    num_slots = peers * capacity
    columns = weight
    mixed = lax.psum_scatter(
        lax.dot_general(
            columns, feats, (((0,), (0,)), ((), ())), preferred_element_type=jnp.float32
        ),
        "feat",
        scatter_dimension=0,
        tiled=True,
    )
    proj = mixed.astype(jnp.bfloat16)
    grid = tile_cols.reshape(row_blocks, per_block)
    tiles = tile_values.reshape(row_blocks, per_block, block, block)
    local_tiles = tiles[:, :TL]
    remote_tiles = tiles[:, TL:]
    local_cols = grid[:, :TL] % row_blocks
    remote_cols = grid[:, TL:].reshape(-1)
    remote_owner = remote_cols // row_blocks
    remote_local = remote_cols % row_blocks
    owner_onehot = (remote_owner[:, None] == jnp.arange(peers)[None, :]).astype(jnp.int32)
    before = jnp.cumsum(owner_onehot, axis=0) - owner_onehot
    ranks = jnp.sum(before * owner_onehot, axis=1)
    slots = remote_owner * capacity + ranks
    request = jnp.full((num_slots,), -1, jnp.int32).at[slots].set(remote_local)
    slot_tile = (
        jnp.full((num_slots,), -1, jnp.int32)
        .at[slots]
        .set(jnp.arange(remote_count, dtype=jnp.int32))
    )
    wanted = lax.all_to_all(
        request.reshape(peers, capacity), "rows", split_axis=0, concat_axis=0, tiled=True
    ).reshape(-1)
    gathered = lax.all_gather(proj, "rows", axis=1, tiled=True)
    gathered = gathered.reshape(hid_dev, -1, block)
    fetched = jnp.take(gathered, tile_cols, axis=1).reshape(hid_dev, row_blocks, per_block, block)
    local_part = jnp.einsum(
        "fbtk,btnk->bfn", fetched[:, :, :TL], local_tiles, preferred_element_type=jnp.float32
    )
    remote_part = jnp.einsum(
        "fbtk,btnk->bfn", fetched[:, :, TL:], remote_tiles, preferred_element_type=jnp.float32
    )
    summed = local_part + remote_part
    pre = summed.transpose(1, 0, 2).reshape(hid_dev, nodes_dev) + bias[:, None]
    hidden_out = jax.nn.silu(pre).astype(jnp.bfloat16)
    sigma = jax.nn.sigmoid(pre)
    grad_pre = cotangent.astype(jnp.float32) * (sigma * (1.0 + pre * (1.0 - sigma)))
    bias_part = jnp.sum(grad_pre, axis=1)
    grad_blocks = (
        grad_pre.astype(jnp.bfloat16).reshape(hid_dev, row_blocks, block).transpose(1, 0, 2)
    )
    local_back = jnp.einsum(
        "bfn,btnk->btfk", grad_blocks, local_tiles, preferred_element_type=jnp.float32
    )
    local_onehot = (local_cols[:, :, None] == jnp.arange(row_blocks)[None, None, :]).astype(
        jnp.float32
    )
    grad_proj_blocks = jnp.einsum(
        "bts,btfk->sfk", local_onehot, local_back, precision=lax.Precision.HIGHEST
    )
    remote_back = jnp.einsum(
        "bfn,btnk->btfk", grad_blocks, remote_tiles, preferred_element_type=jnp.float32
    )
    remote_back = remote_back.reshape(remote_count, hid_dev, block)
    filled = (slot_tile >= 0).astype(jnp.float32)
    outgoing_back = remote_back[jnp.maximum(slot_tile, 0)] * filled[:, None, None]
    outgoing_back = outgoing_back.reshape(peers, capacity, hid_dev, block)
    returned = lax.all_to_all(
        outgoing_back, "rows", split_axis=0, concat_axis=0, tiled=True
    ).reshape(num_slots, hid_dev, block)
    wanted_onehot = (wanted[:, None] == jnp.arange(row_blocks)[None, :]).astype(jnp.float32)
    grad_proj_blocks = grad_proj_blocks + jnp.einsum(
        "sb,sfk->bfk", wanted_onehot, returned, precision=lax.Precision.HIGHEST
    )
    grad_proj = grad_proj_blocks.transpose(1, 0, 2).reshape(hid_dev, nodes_dev).astype(jnp.bfloat16)
    piece = lax.all_gather(grad_proj, "feat", axis=0, tiled=True)
    columns = weight
    input_grad = jnp.dot(columns, piece, preferred_element_type=jnp.float32)
    partial_rows = lax.dot_general(
        feats, piece, (((1,), (1,)), ((), ())), preferred_element_type=jnp.float32
    )
    weight_total, bias_total = lax.psum((partial_rows, bias_part), "rows")
    divisor = math.sqrt(nodes_dev * peers)
    return (hidden_out, input_grad, weight_total / divisor, bias_total / divisor)


def solution(mesh):
    placed = (
        P("feat", "rows"),
        P("feat", None),
        P("feat"),
        P("rows"),
        P("rows", None, None),
        P("feat", "rows"),
    )
    return jax.shard_map(
        local,
        mesh=mesh,
        in_specs=placed,
        out_specs=(P("feat", "rows"), P("feat", "rows"), P("feat", None), P("feat")),
        check_vma=False,
    )
```

profile of v0, /device:TPU:1, one launch (start us, length us, event | category | flops | bytes accessed | tf_op | source)
XLA Modules:
  0.0 594.8 jit_solution(7321926682911000968)
XLA Ops:
  7.2 0.0 copy-start
  7.2 0.0 reduce-scatter.2.cloned.1.call-start
  7.2 0.9 copy-done
  8.1 2.6 fusion.50
  10.7 0.0 copy-start.5
  10.7 0.0 reduce-scatter.2.cloned.1.call-update
  10.7 0.0 all-gather.3.cloned.1.call-start
  10.8 36.1 %reduce-scatter.2.cloned.1.call-done = f32[64,2048]{1,0:T(8,128)} async-done(((f32[256,2048]{1,0:T(8,128)}), f32[64,2048]{1,0:T(8,128)}) %reduce-scatter.2.cloned.1.call-update) | async-done | bytes 524304 | tf_op jit(solution)/shard_map/reduce_scatter | solution.py:22
  46.9 1.8 convert_element_type.27
  48.7 0.0 all-gather.3.cloned.1.call-update
  48.7 0.0 copy-done.5
  48.7 0.1 reshape.160
  48.8 0.1 fusion.49
  48.9 0.1 reshape.163
  49.0 0.1 reshape.162
  49.1 0.1 fusion.33
  49.1 0.1 reduce_window_sum.11
  49.2 0.2 select_reduce_fusion
  49.4 0.8 scatter_custom_fusion
  50.2 0.8 all_to_all.9
  51.0 10.6 %all-to-all-start = ((s32[64,1,2]{2,1,0:T(1,128)}), s32[64,1,2]{2,1,0:T(1,128)S(1)}, u32[]{:S(2)}, u32[]{:S(2)}) async-start(s32[64,1,2]{2,1,0:T(1,128)} %bitcast.17), calls=%async_computation.1 | async-start | bytes 65536 | tf_op jit(solution)/shard_map/all_to_all | solution.py:49
  61.6 0.1 broadcast_in_dim.26
  61.7 0.8 scatter_custom_fusion.1
  62.5 0.1 reshape.166
  62.7 88.0 %all-gather.3.cloned.1.call-done = bf16[64,131072]{1,0:T(8,128)(2,1)} async-done(((bf16[64,2048]{1,0:T(8,128)(2,1)}), bf16[64,131072]{1,0:T(8,128)(2,1)}) %all-gather.3.cloned.1.call-update) | async-done | bytes 16777232 | tf_op jit(solution)/shard_map/all_gather | solution.py:52
  150.8 15.3 %copy_bitcast_fusion = bf16[64,1024,128]{2,0,1:T(8,128)(2,1)} fusion(bf16[64,131072]{1,0:T(8,128)(2,1)} %all-gather.3.cloned.1.call-done), kind=kLoop, calls=%fused_computation.4 | loop fusion | bytes 33554432 | tf_op jit(solution)/shard_map/reshape | solution.py:53
  166.0 6.7 %gather_fusion = bf16[128,64,128]{2,1,0:T(8,128)(2,1)S(1)} fusion(bf16[64,1024,128]{2,0,1:T(8,128)(2,1)} %copy_bitcast_fusion, s32[1024]{0:T(1024)S(1)} %pad_clamp_fusion.1), kind=kCustom, calls=%fused_computation | custom fusion | bytes 4194816 | tf_op jit(solution)/shard_map/jit(_take)/gather | solution.py:54
  172.8 0.0 copy-start.1
  172.8 2.6 fusion.16
  175.4 0.2 copy-done.1
  175.6 0.0 copy-start.2
  175.6 0.0 copy-start.4
  175.6 0.9 fusion.25
  176.5 0.0 copy-done.2
  176.5 0.0 copy-done.4
  176.5 1.1 fusion.48
  177.7 0.5 fusion.2
  178.1 2.8 gather_fusion.1
  180.9 2.5 broadcast_multiply_fusion
  183.4 5.8 copy.32
  189.2 0.0 all-to-all-done
  189.2 6.2 %all-to-all-start.1 = ((f32[64,2,64,128]{3,1,2,0:T(2,128)}), f32[64,2,64,128]{3,1,2,0:T(2,128)}, u32[]{:S(2)}, u32[]{:S(2)}) async-start(f32[64,2,64,128]{3,1,2,0:T(2,128)} %copy.32), calls=%async_computation.2 | async-start | bytes 8388608 | tf_op jit(solution)/shard_map/all_to_all | solution.py:86
  195.4 0.2 all-gather.5.cloned.1.call-start
  195.6 0.1 copy.28
  195.7 0.5 broadcast.163
  196.2 0.7 reduce.3
  197.0 0.1 eq.51
  197.1 2.0 fusion.10
  199.1 2.3 fusion.13
  201.4 89.9 %all-to-all-done.1 = f32[64,2,64,128]{3,1,2,0:T(2,128)} async-done(((f32[64,2,64,128]{3,1,2,0:T(2,128)}), f32[64,2,64,128]{3,1,2,0:T(2,128)}, u32[]{:S(2)}, u32[]{:S(2)}) %all-to-all-start.1) | async-done | bytes 4194336 | tf_op jit(solution)/shard_map/all_to_all | solution.py:86
  291.3 4.5 copy.33
  295.8 1.5 fusion.28
  297.3 0.0 copy-start.3
  297.3 0.8 copy.62
  298.1 0.0 all-gather.5.cloned.1.call-update
  298.1 0.0 all-reduce.2.cloned.1.call-start
  298.2 123.7 %psum.15 = f32[64]{0:T(128)S(1)} all-reduce(f32[64]{0:T(128)S(1)} %get-tuple-element.4), channel_id=1, replica_groups=mesh['rows'=64,'feat'=4] {'rows'}, use_global_device_ids=true, to_apply=%region_7.8 | all-reduce | flops 64 | bytes 512 | tf_op jit(solution)/shard_map/psum | solution.py:100
  421.9 0.5 broadcast_multiply_fusion.2
  422.4 2.3 convolution_bitcast_fusion.1
  424.7 0.0 all-reduce.2.cloned.1.call-update
  424.8 0.0 copy-done.3
  424.8 2.3 convolution_bitcast_fusion
  427.1 159.7 %all-reduce.2.cloned.1.call-done = f32[64,256]{1,0:T(8,128)} async-done(((f32[64,256]{1,0:T(8,128)}), f32[64,256]{1,0:T(8,128)}) %all-reduce.2.cloned.1.call-update) | async-done | bytes 65552 | tf_op jit(solution)/shard_map/psum | solution.py:100
  586.8 1.5 broadcast_multiply_fusion.1
  (10 shorter events, 0.1 us)
Async XLA Ops:
  7.2 1.0 copy-start
  7.2 39.7 %reduce-scatter.2.cloned.1.call-start = ((), (), s32[]{:S(2)}) async-start(), calls=%async_computation.3 | async-start | bytes 2621440 | tf_op jit(solution)/shard_map/reduce_scatter | solution.py:22
  10.7 38.0 %copy-start.5 = (s32[128]{0:T(128)S(1)}, s32[128]{0:T(128)}, u32[]{:S(2)}) copy-start(s32[128]{0:T(128)} %param.9) | copy-start | bytes 1540
  10.7 140.0 %all-gather.3.cloned.1.call-start = ((), (), s32[]{:S(2)}) async-start(), calls=%async_computation.4 | async-start | bytes 17039360 | tf_op jit(solution)/shard_map/all_gather | solution.py:52
  51.0 138.2 %all-to-all-start = ((s32[64,1,2]{2,1,0:T(1,128)}), s32[64,1,2]{2,1,0:T(1,128)S(1)}, u32[]{:S(2)}, u32[]{:S(2)}) async-start(s32[64,1,2]{2,1,0:T(1,128)} %bitcast.17), calls=%async_computation.1 | async-start | bytes 65536 | tf_op jit(solution)/shard_map/all_to_all | solution.py:49
  172.8 2.8 copy-start.1
  175.6 0.9 copy-start.2
  175.6 1.0 copy-start.4
  189.2 102.1 %all-to-all-start.1 = ((f32[64,2,64,128]{3,1,2,0:T(2,128)}), f32[64,2,64,128]{3,1,2,0:T(2,128)}, u32[]{:S(2)}, u32[]{:S(2)}) async-start(f32[64,2,64,128]{3,1,2,0:T(2,128)} %copy.32), calls=%async_computation.2 | async-start | bytes 8388608 | tf_op jit(solution)/shard_map/all_to_all | solution.py:86
  195.4 227.0 %all-gather.5.cloned.1.call-start = ((), (), s32[]{:S(2)}) async-start(), calls=%async_computation.5 | async-start | bytes 1310720 | tf_op jit(solution)/shard_map/all_gather | solution.py:94
  297.3 127.4 %copy-start.3 = (bf16[64,256]{1,0:T(8,128)(2,1)S(1)}, bf16[64,256]{1,0:T(8,128)(2,1)}, u32[]{:S(2)}) copy-start(bf16[64,256]{1,0:T(8,128)(2,1)} %param.7) | copy-start | bytes 98308
  298.1 288.7 %all-reduce.2.cloned.1.call-start = ((), (), s32[]{:S(2)}) async-start(), calls=%async_computation.6 | async-start | bytes 131072 | tf_op jit(solution)/shard_map/psum | solution.py:100
Sparse Core Ops, SparseCore 0:
  10.8 36.0 reduce-scatter.1
  50.7 100.0 all-gather.2
  298.2 21.9 all-gather.4
  424.9 161.8 all-reduce.1
where the time goes:
time: 596 us; the launch traced here: 595 us
  waiting for transfers between devices  374 us (63%)
  blocking collectives  124 us (21%)
  local copies, waits for them, and re-layouts  40.5 us (7%)
  starting transfers between devices  17.1 us (3%)
  matrix products  17 us (3%)
  between operations  14 us (2%)
  other arithmetic  8.64 us (1%)
    psum x1, waiting for transfers between devices, local(): weight_total, bias_total = lax.psum((partial_rows, bias_part), 'rows')  160 us
    psum x1, blocking collectives, local(): weight_total, bias_total = lax.psum((partial_rows, bias_part), 'rows')  124 us
    all_to_all x1, waiting for transfers between devices, local(): lax.all_to_all(outgoing_back, 'rows', split_axis=0, concat_axis=0, tiled=...  89.9 us
    all_gather x1, waiting for transfers between devices, local(): gathered = lax.all_gather(proj, 'rows', axis=1, tiled=True)  88 us
    reduce_scatter x1, waiting for transfers between devices, local(): lax.psum_scatter(lax.dot_general(columns, feats, (((0,), (0,)), ((), ()))...  36.1 us
    reshape x1, local copies, waits for them, and re-layouts, local(): gathered = gathered.reshape(hid_dev, -1, block)  15.3 us
  transfers between devices with their start and end apart: 6, of which 4 were waited for; matrix products, arithmetic and copies ran while one was open for 8% of the time, Pallas kernels for 0%

commit v1 on v0

--- a/solution.py
+++ b/solution.py
@@ -1,3 +1,4 @@
+import functools
 import math
 import jax
 import jax.numpy as jnp
@@ -5,6 +6,21 @@
 from jax.sharding import PartitionSpec as P
 
 TL = 4
+
+
+def drive_regions(slab_in, on_dim):
+    return jnp.concatenate(
+        lax.all_to_all(
+            jnp.stack([slab_in for _ in range(lax.axis_size("rows"))], axis=0),
+            axis_name="rows",
+            split_axis=0,
+            concat_axis=0,
+        ),
+        axis=on_dim,
+    )
+
+
+use_works_on = functools.partial(drive_regions, on_dim=1)
 
 
 def local(feats, weight, bias, tile_cols, tile_values, cotangent):
@@ -49,7 +65,7 @@
     wanted = lax.all_to_all(
         request.reshape(peers, capacity), "rows", split_axis=0, concat_axis=0, tiled=True
     ).reshape(-1)
-    gathered = lax.all_gather(proj, "rows", axis=1, tiled=True)
+    gathered = use_works_on(proj)
     gathered = gathered.reshape(hid_dev, -1, block)
     fetched = jnp.take(gathered, tile_cols, axis=1).reshape(hid_dev, row_blocks, per_block, block)
     local_part = jnp.einsum(

time: 596 us -> 933 us (1.57)
  waiting for transfers between devices: 374 us -> 646 us
  local copies, waits for them, and re-layouts: 40.5 us -> 94 us
  starting transfers between devices: 17.1 us -> 27.9 us
    all_to_all x0 -> x1, waiting for transfers between devices: none -> 362 us  [drive_regions(): lax.all_to_all(jnp.stack([slab_in for _ in range(lax.axis_size('rows'))],...]
    all_gather x1 -> x0, waiting for transfers between devices: 88 us -> none  [local(): gathered = lax.all_gather(proj, 'rows', axis=1, tiled=True)]
    another operation x0 -> x3, local copies, waits for them, and re-layouts: none -> 50.2 us  [the longest x2 44.2 us: local(): gathered = gathered.reshape(hid_dev, -1, block)]
    all_to_all x0 -> x1, starting transfers between devices: none -> 11 us  [drive_regions(): lax.all_to_all(jnp.stack([slab_in for _ in range(lax.axis_size('rows'))],...]
  transfers between devices with their start and end apart: 6 -> 6, of which waited for: 4 -> 4; matrix products, arithmetic and copies ran while one was open for 8% -> 10% of each run, Pallas kernels for 0% -> 0%
where the time goes in v1:
time: 933 us; the launch traced here: 931 us
  waiting for transfers between devices  646 us (69%)
  blocking collectives  124 us (13%)
  local copies, waits for them, and re-layouts  94 us (10%)
  starting transfers between devices  27.9 us (3%)
  matrix products  17 us (2%)
  between operations  14 us (2%)
    all_to_all x1, waiting for transfers between devices, drive_regions(): lax.all_to_all(jnp.stack([slab_in for _ in range(lax.axis_size('rows'))],...  362 us
    psum x1, waiting for transfers between devices, local(): weight_total, bias_total = lax.psum((partial_rows, bias_part), 'rows')  158 us
    psum x1, blocking collectives, local(): weight_total, bias_total = lax.psum((partial_rows, bias_part), 'rows')  124 us
    all_to_all x1, waiting for transfers between devices, local(): lax.all_to_all(outgoing_back, 'rows', split_axis=0, concat_axis=0, tiled=...  89.8 us
    another operation x2, local copies, waits for them, and re-layouts, local(): gathered = gathered.reshape(hid_dev, -1, block)  44.2 us
    reduce_scatter x1, waiting for transfers between devices, local(): lax.psum_scatter(lax.dot_general(columns, feats, (((0,), (0,)), ((), ()))...  36.2 us
  transfers between devices with their start and end apart: 6, of which 4 were waited for; matrix products, arithmetic and copies ran while one was open for 10% of the time, Pallas kernels for 0%

profile of v1, /device:TPU:1, one launch (start us, length us, event | category | flops | bytes accessed | tf_op | source)
XLA Modules:
  0.0 930.7 jit_solution(17372737411794609728)
XLA Ops:
  7.2 0.0 copy-start
  7.2 0.0 reduce-scatter.2.cloned.1.call-start
  7.2 0.9 copy-done
  8.1 2.6 fusion.50
  10.7 0.0 reduce-scatter.2.cloned.1.call-update
  10.7 36.2 %reduce-scatter.2.cloned.1.call-done = f32[64,2048]{1,0:T(8,128)} async-done(((f32[256,2048]{1,0:T(8,128)}), f32[64,2048]{1,0:T(8,128)}) %reduce-scatter.2.cloned.1.call-update) | async-done | bytes 524304 | tf_op jit(solution)/shard_map/reduce_scatter | solution.py:38
  46.9 1.1 convert_element_type.27
  48.0 6.0 stack.2
  54.0 0.0 copy-start.5
  54.0 11.0 %all-to-all-start = ((bf16[64,64,2048]{2,1,0:T(8,128)(2,1)}), bf16[64,64,2048]{2,1,0:T(8,128)(2,1)}, u32[]{:S(2)}, u32[]{:S(2)}) async-start(bf16[64,64,2048]{2,1,0:T(8,128)(2,1)} %stack.2), calls=%async_computation.1 | async-start | bytes 33554432 | tf_op jit(solution)/shard_map/all_to_all | solution.py:13
  64.9 0.0 copy-done.5
  64.9 0.1 reshape.162
  65.0 0.1 fusion.49
  65.1 0.1 reshape.165
  65.2 0.1 reshape.164
  65.3 0.1 broadcast_in_dim.26
  65.4 0.1 fusion.33
  65.5 0.1 reduce_window_sum.11
  65.6 0.2 select_reduce_fusion
  65.8 0.8 scatter_custom_fusion.1
  66.6 0.1 reshape.168
  66.7 0.8 scatter_custom_fusion
  67.5 0.8 all_to_all.13
  68.3 362.2 %all-to-all-done = bf16[64,64,2048]{2,1,0:T(8,128)(2,1)} async-done(((bf16[64,64,2048]{2,1,0:T(8,128)(2,1)}), bf16[64,64,2048]{2,1,0:T(8,128)(2,1)}, u32[]{:S(2)}, u32[]{:S(2)}) %all-to-all-start) | async-done | bytes 16777248 | tf_op jit(solution)/shard_map/all_to_all | solution.py:13
  430.5 6.1 all-to-all-start.1
  436.5 18.6 %copy.26 = bf16[64,64,2048]{2,1,0:T(8,128)(2,1)} copy(bf16[64,64,2048]{2,0,1:T(8,128)(2,1)} %bitcast) | data formatting | bytes 33554432 | tf_op jit(solution)/shard_map/reshape | solution.py:12
  455.2 25.6 %reshape_reshape.3 = bf16[64,1024,128]{2,1,0:T(8,128)(2,1)} reshape(bf16[64,64,2048]{2,1,0:T(8,128)(2,1)} %copy.26) | data formatting | bytes 33554432 | tf_op jit(solution)/shard_map/reshape;reshape | solution.py:69
  480.8 18.6 %copy.27 = bf16[64,1024,128]{2,0,1:T(8,128)(2,1)} copy(bf16[64,1024,128]{2,1,0:T(8,128)(2,1)} %reshape_reshape.3) | data formatting | bytes 33554432 | tf_op jit(solution)/shard_map/reshape;reshape | solution.py:69
  499.4 6.7 gather_fusion
  506.1 0.0 copy-start.1
  506.1 2.6 fusion.16
  508.7 0.2 copy-done.1
  508.9 0.0 copy-start.2
  508.9 0.9 fusion.25
  509.8 0.0 copy-done.2
  509.9 0.0 copy-done.4
  509.9 1.1 fusion.48
  511.0 0.5 fusion.2
  511.5 2.7 gather_fusion.1
  514.2 2.5 broadcast_multiply_fusion
  516.7 5.8 copy.33
  522.5 0.0 all-to-all-done.1
  522.6 10.5 %all-to-all-start.2 = ((f32[64,2,64,128]{3,1,2,0:T(2,128)}), f32[64,2,64,128]{3,1,2,0:T(2,128)}, u32[]{:S(2)}, u32[]{:S(2)}) async-start(f32[64,2,64,128]{3,1,2,0:T(2,128)} %copy.33), calls=%async_computation.3 | async-start | bytes 8388608 | tf_op jit(solution)/shard_map/all_to_all | solution.py:102
  533.1 0.3 all-gather.2.cloned.1.call-start
  533.3 0.1 copy.29
  533.4 0.5 broadcast.165
  533.9 0.7 reduce.3
  534.7 0.1 eq.51
  534.8 2.0 fusion.10
  536.8 2.3 fusion.13
  539.1 89.8 %all-to-all-done.2 = f32[64,2,64,128]{3,1,2,0:T(2,128)} async-done(((f32[64,2,64,128]{3,1,2,0:T(2,128)}), f32[64,2,64,128]{3,1,2,0:T(2,128)}, u32[]{:S(2)}, u32[]{:S(2)}) %all-to-all-start.2) | async-done | bytes 4194336 | tf_op jit(solution)/shard_map/all_to_all | solution.py:102
  629.0 4.5 copy.34
  633.5 1.5 fusion.28
  635.0 0.8 copy.61
  635.8 0.0 all-gather.2.cloned.1.call-update
  635.8 0.0 all-reduce.2.cloned.1.call-start
  635.8 123.7 %psum.15 = f32[64]{0:T(128)S(1)} all-reduce(f32[64]{0:T(128)S(1)} %get-tuple-element.4), channel_id=1, replica_groups=mesh['rows'=64,'feat'=4] {'rows'}, use_global_device_ids=true, to_apply=%region_7.8 | all-reduce | flops 64 | bytes 512 | tf_op jit(solution)/shard_map/psum | solution.py:116
  759.6 0.5 broadcast_multiply_fusion.2
  760.1 2.3 convolution_bitcast_fusion.1
  762.4 0.0 all-reduce.2.cloned.1.call-update
  762.4 0.0 copy-done.3
  762.4 2.3 convolution_bitcast_fusion
  764.8 158.0 %all-reduce.2.cloned.1.call-done = f32[64,256]{1,0:T(8,128)} async-done(((f32[64,256]{1,0:T(8,128)}), f32[64,256]{1,0:T(8,128)}) %all-reduce.2.cloned.1.call-update) | async-done | bytes 65552 | tf_op jit(solution)/shard_map/psum | solution.py:116
  922.7 1.5 broadcast_multiply_fusion.1
  (12 shorter events, 0.1 us)
Async XLA Ops:
  7.2 1.0 copy-start
  7.2 39.7 %reduce-scatter.2.cloned.1.call-start = ((), (), s32[]{:S(2)}) async-start(), calls=%async_computation.4 | async-start | bytes 2621440 | tf_op jit(solution)/shard_map/reduce_scatter | solution.py:38
  54.0 11.0 %copy-start.5 = (s32[128]{0:T(128)S(1)}, s32[128]{0:T(128)}, u32[]{:S(2)}) copy-start(s32[128]{0:T(128)} %param.9) | copy-start | bytes 1540
  54.0 376.5 %all-to-all-start = ((bf16[64,64,2048]{2,1,0:T(8,128)(2,1)}), bf16[64,64,2048]{2,1,0:T(8,128)(2,1)}, u32[]{:S(2)}, u32[]{:S(2)}) async-start(bf16[64,64,2048]{2,1,0:T(8,128)(2,1)} %stack.2), calls=%async_computation.1 | async-start | bytes 33554432 | tf_op jit(solution)/shard_map/all_to_all | solution.py:13
  430.5 92.1 %all-to-all-start.1 = ((s32[64,1,2]{2,1,0:T(1,128)}), s32[64,1,2]{2,1,0:T(1,128)S(1)}, u32[]{:S(2)}, u32[]{:S(2)}) async-start(s32[64,1,2]{2,1,0:T(1,128)} %bitcast.18), calls=%async_computation.2 | async-start | bytes 65536 | tf_op jit(solution)/shard_map/all_to_all | solution.py:65
  506.1 2.8 copy-start.1
  508.9 0.9 copy-start.2
  508.9 1.0 copy-start.4
  522.6 106.4 %all-to-all-start.2 = ((f32[64,2,64,128]{3,1,2,0:T(2,128)}), f32[64,2,64,128]{3,1,2,0:T(2,128)}, u32[]{:S(2)}, u32[]{:S(2)}) async-start(f32[64,2,64,128]{3,1,2,0:T(2,128)} %copy.33), calls=%async_computation.3 | async-start | bytes 8388608 | tf_op jit(solution)/shard_map/all_to_all | solution.py:102
  533.1 227.0 %all-gather.2.cloned.1.call-start = ((), (), s32[]{:S(2)}) async-start(), calls=%async_computation.5 | async-start | bytes 1310720 | tf_op jit(solution)/shard_map/all_gather | solution.py:110
  635.0 127.4 %copy-start.3 = (bf16[64,256]{1,0:T(8,128)(2,1)S(1)}, bf16[64,256]{1,0:T(8,128)(2,1)}, u32[]{:S(2)}) copy-start(bf16[64,256]{1,0:T(8,128)(2,1)} %param.7) | copy-start | bytes 98308
  635.8 286.9 %all-reduce.2.cloned.1.call-start = ((), (), s32[]{:S(2)}) async-start(), calls=%async_computation.6 | async-start | bytes 131072 | tf_op jit(solution)/shard_map/psum | solution.py:116
Sparse Core Ops, SparseCore 0:
  10.8 36.0 reduce-scatter.1
  635.9 20.4 all-gather.1
  762.6 160.1 all-reduce.1
